TPU v7x, 512 devices: a whole 4x4x16 slice. The times are simulated.
512 devices in a mesh: swath: 32 (over z, core), chan: 16 (over x, y).
Axes of the slice: x: 4, y: 4, z: 16, core: 2. Of those that a mesh axis runs over, the one named last changes fastest.
Arguments:
- grid_profiles: bfloat16 [32768, 256], P('swath'), may hold values from -6 to 6
- send_lists: int32 [32, 32, 128], P('swath'), may hold values from 0 to 1023
- counts: int32 [32, 32], P('swath'), may hold values from 1 to 128, as said below
- angle_index: int32 [128], replicated, may hold values from 0 to 7
- jacobian: bfloat16 [3, 256, 608], P(None, None, 'chan'), may hold values from -0.375 to 0.375
- observed: bfloat16 [608, 131072], P('chan', 'swath'), may hold values from -6 to 6
- kappa: float32 [2, 608], P(None, 'chan'), may hold values from 0.04 to 0.24
- factor: bfloat16 [608, 608], P('chan')
Outputs:
- weighted: float32 [608, 131072], P('chan', 'swath')
Inputs may be any that keep to these rules, and one draw needn't show every extreme that they name: `counts`: some receiver gets 128 live slots from every sender; every entry is at least one.
All inputs are finite; a program needn't handle non-finite values.
Results may differ from a plain program's by a relative error of at most 0.0029.
Values may be sent and summed in bfloat16 or wider, within the bound.
A program may use at most 64 MiB of HBM per device.

v0:
```python
import math
import jax
import jax.numpy as jnp
from jax import lax
from jax.sharding import PartitionSpec as P

XTRACK = 128
NANG = 8
max_zenith = math.pi / 3.0


def extended_2(block, sides, width):
    for axis, dim in sides:
        count = lax.axis_size(axis)
        forward = [(i, i + 1) for i in range(count - 1)]
        backward = [(target, source) for source, target in forward]
        low = lax.ppermute(
            lax.slice_in_dim(block, block.shape[dim] - width, None, axis=dim), axis, forward
        )
        high = lax.ppermute(lax.slice_in_dim(block, 0, width, axis=dim), axis, backward)
        block = jnp.concatenate([low, block, high], axis=dim)
    return block


def diffuse_once(extended, along_rate, cross_rate):
    center = extended[:, 1:-1]
    along_sum = extended[:, 2:] + extended[:, :-2] - 2.0 * center
    side_pad = jnp.pad(center, ((0, 0), (0, 0), (1, 1)))
    cross_sum = side_pad[:, :, 2:] + side_pad[:, :, :-2] - 2.0 * center
    return center + along_rate * along_sum + cross_rate * cross_sum


def line_rims(smooth_field):
    return extended_2(smooth_field, (("swath", 1),), 1)


def on_device(grid_profiles, send_lists, counts, angle_index, jacobian, observed, kappa, factor):
    slot_rows = send_lists[0]
    slots = slot_rows.shape[1]
    own_chan = observed.shape[0]
    pixel_count = observed.shape[1]
    line_count = pixel_count // XTRACK
    live_slot = jnp.arange(slots, dtype=jnp.int32)[None, :] < counts[0][:, None]
    zero_value = jnp.zeros((), grid_profiles.dtype)
    outgoing = jnp.where(live_slot[:, :, None], grid_profiles[slot_rows], zero_value)
    incoming = lax.all_to_all(outgoing, "swath", split_axis=0, concat_axis=0, tiled=True)
    pixel_profiles = incoming.reshape(pixel_count, grid_profiles.shape[1])
    model = jnp.einsum("mkc,pk->mcp", jacobian, pixel_profiles, preferred_element_type=jnp.float32)
    zenith = angle_index.astype(jnp.float32) * (max_zenith / (NANG - 1))
    slant_path = 1.0 / jnp.cos(zenith) - 1.0
    model = model.reshape(3, own_chan, line_count, XTRACK)
    departure = observed.astype(jnp.float32).reshape(own_chan, line_count, XTRACK) - (
        model[0] + slant_path * model[1] + slant_path * slant_path * model[2]
    )
    along_rate = kappa[0][:, None, None]
    cross_rate = kappa[1][:, None, None]
    smooth_field = departure
    for sweep in range(3):
        smooth_field = diffuse_once(line_rims(smooth_field), along_rate, cross_rate)
    smoothed = smooth_field.reshape(own_chan, pixel_count).astype(jnp.bfloat16)
    return jnp.dot(
        factor,
        lax.all_gather(smoothed, "chan", axis=0, tiled=True),
        preferred_element_type=jnp.float32,
    )


def solution(mesh):
    in_specs = (
        P("swath", None),
        P("swath", None, None),
        P("swath", None),
        P(),
        P(None, None, "chan"),
        P("chan", "swath"),
        P(None, "chan"),
        P("chan", None),
    )
    out_specs = P("chan", "swath")
    return jax.shard_map(
        on_device, mesh=mesh, in_specs=in_specs, out_specs=out_specs, check_vma=False
    )
```

profile of v0, /device:TPU:1, one launch (start us, length us, event | category | flops | bytes accessed | tf_op | source)
XLA Modules:
  0.0 252.0 jit_solution(1715933017502331585)
XLA Ops:
  6.5 0.8 iota_compare_fusion
  7.3 0.7 fusion.29
  8.1 14.6 %gather_fusion = bf16[4096,256]{1,0:T(8,128)(2,1)S(1)} fusion(bf16[1024,256]{1,0:T(8,128)(2,1)S(1)} %copy-done, s32[4096]{0:T(1024)S(1)} %fusion.29), kind=kCustom, calls=%fused_computation | custom fusion | bytes 4210688 | tf_op jit(solution)/shard_map/gather | solution.py:45
  22.7 1.7 broadcast_select_fusion
  24.4 16.9 %all-to-all-start = ((bf16[32,128,256]{2,1,0:T(8,128)(2,1)}), bf16[32,128,256]{2,1,0:T(8,128)(2,1)S(1)}, u32[]{:S(2)}, u32[]{:S(2)}) async-start(bf16[32,128,256]{2,1,0:T(8,128)(2,1)} %broadcast_select_fusion), calls=%async_computation | async-start | bytes 4194304 | tf_op jit(solution)/shard_map/all_to_all | solution.py:46
  41.5 0.4 copy-done.5
  42.0 97.9 %all-to-all-done = bf16[32,128,256]{2,1,0:T(8,128)(2,1)S(1)} async-done(((bf16[32,128,256]{2,1,0:T(8,128)(2,1)}), bf16[32,128,256]{2,1,0:T(8,128)(2,1)S(1)}, u32[]{:S(2)}, u32[]{:S(2)}) %all-to-all-start) | async-done | bytes 2097184 | tf_op jit(solution)/shard_map/all_to_all | solution.py:46
  139.9 0.8 convolution_bitcast_fusion
  141.6 2.8 %collective-permute-start = (f32[38,1,128]{2,1,0:T(1,128)S(1)}, f32[38,1,128]{2,1,0:T(1,128)S(1)}, u32[]{:S(2)}, u32[]{:S(2)}) collective-permute-start(f32[38,1,128]{2,1,0:T(1,128)S(1)} %get-tuple-element.14), channel_id=1, source_target_pairs={{16,0},{32,16},{48,32},{64,48},{80,64},{96,80},{112,96},{128,112},... | collective-permute-start | bytes 58376 | tf_op jit(solution)/shard_map/ppermute | solution.py:20
  144.3 4.2 %collective-permute-start.1 = (f32[38,1,128]{2,1,0:T(1,128)S(1)}, f32[38,1,128]{2,1,0:T(1,128)S(1)}, u32[]{:S(2)}, u32[]{:S(2)}) collective-permute-start(f32[38,1,128]{2,1,0:T(1,128)S(1)} %get-tuple-element.15), channel_id=1, source_target_pairs={{0,16},{16,32},{32,48},{48,64},{64,80},{80,96},{96,112},{112,128},... | collective-permute-start | bytes 58376 | tf_op jit(solution)/shard_map/ppermute | solution.py:17
  148.6 0.8 collective-permute-done.1
  149.4 0.5 fusion.3
  150.0 1.9 collective-permute-start.2
  151.9 4.2 %collective-permute-start.3 = (f32[38,1,128]{2,1,0:T(1,128)S(1)}, f32[38,1,128]{2,1,0:T(1,128)S(1)}, u32[]{:S(2)}, u32[]{:S(2)}) collective-permute-start(f32[38,1,128]{2,1,0:T(1,128)S(1)} %get-tuple-element.13), channel_id=1, source_target_pairs={{0,16},{16,32},{32,48},{48,64},{64,80},{80,96},{96,112},{112,128},... | collective-permute-start | bytes 58376 | tf_op jit(solution)/shard_map/ppermute | solution.py:17
  156.2 0.9 collective-permute-done.3
  157.0 0.5 fusion.7
  157.6 1.9 collective-permute-start.4
  159.5 4.2 %collective-permute-start.5 = (f32[38,1,128]{2,1,0:T(1,128)S(1)}, f32[38,1,128]{2,1,0:T(1,128)S(1)}, u32[]{:S(2)}, u32[]{:S(2)}) collective-permute-start(f32[38,1,128]{2,1,0:T(1,128)S(1)} %get-tuple-element.11), channel_id=1, source_target_pairs={{0,16},{16,32},{32,48},{48,64},{64,80},{80,96},{96,112},{112,128},... | collective-permute-start | bytes 58376 | tf_op jit(solution)/shard_map/ppermute | solution.py:17
  163.8 0.9 collective-permute-done.5
  164.6 0.6 fusion.12
  165.2 0.9 reshape.88
  166.2 69.0 %all-gather.3.cloned.1.call-done = bf16[16,38,4096]{2,1,0:T(8,128)(2,1)} async-done(((bf16[1,38,4096]{2,1,0:T(8,128)(2,1)}), bf16[16,38,4096]{2,1,0:T(8,128)(2,1)}) %all-gather.3.cloned.1.call-update) | async-done | bytes 4980752 | tf_op jit(solution)/shard_map/all_gather | solution.py:63
  235.2 5.7 %reshape.89 = bf16[608,4096]{1,0:T(8,128)(2,1)} reshape(bf16[16,38,4096]{2,1,0:T(8,128)(2,1)} %all-gather.3.cloned.1.call-done) | data formatting | bytes 9961472
  240.9 4.2 %convolution_bitcast_fusion.1 = f32[38,4096]{1,0:T(8,128)} fusion(bf16[608,4096]{1,0:T(8,128)(2,1)} %reshape.89, bf16[38,608]{1,0:T(8,128)(2,1)S(1)} %copy-done.3), kind=kOutput, calls=%fused_computation.2 | convolution fusion | flops 189267968 | bytes 5649536 | tf_op jit(solution)/shard_map/dot_general | solution.py:61
  (28 shorter events, 1.2 us)
Async XLA Ops:
  6.5 1.5 copy-start
  24.4 17.0 %copy-start.1 = (bf16[38,4096]{1,0:T(8,128)(2,1)S(1)}, bf16[38,4096]{1,0:T(8,128)(2,1)}, u32[]{:S(2)}) copy-start(bf16[38,4096]{1,0:T(8,128)(2,1)} %param.13) | copy-start | bytes 933892
  24.4 115.5 %all-to-all-start = ((bf16[32,128,256]{2,1,0:T(8,128)(2,1)}), bf16[32,128,256]{2,1,0:T(8,128)(2,1)S(1)}, u32[]{:S(2)}, u32[]{:S(2)}) async-start(bf16[32,128,256]{2,1,0:T(8,128)(2,1)} %broadcast_select_fusion), calls=%async_computation | async-start | bytes 4194304 | tf_op jit(solution)/shard_map/all_to_all | solution.py:46
  41.2 0.7 copy-start.5
  41.3 98.6 %copy-start.2 = (bf16[3,256,38]{1,2,0:T(8,128)(2,1)S(1)}, bf16[3,256,38]{1,2,0:T(8,128)(2,1)}, u32[]{:S(2)}) copy-start(bf16[3,256,38]{1,2,0:T(8,128)(2,1)} %param.12) | copy-start | bytes 175108
  41.3 193.9 %all-gather.3.cloned.1.call-start = ((), (), s32[]{:S(2)}) async-start(), calls=%async_computation.1 | async-start | bytes 5570560 | tf_op jit(solution)/shard_map/all_gather | solution.py:63
  141.1 7.5 %copy-start.4 = (f32[2,38]{1,0:T(2,128)S(1)}, f32[2,38]{1,0:T(2,128)}, u32[]{:S(2)}) copy-start(f32[2,38]{1,0:T(2,128)} %param.14) | copy-start | bytes 916
  141.6 7.0 %collective-permute-start = (f32[38,1,128]{2,1,0:T(1,128)S(1)}, f32[38,1,128]{2,1,0:T(1,128)S(1)}, u32[]{:S(2)}, u32[]{:S(2)}) collective-permute-start(f32[38,1,128]{2,1,0:T(1,128)S(1)} %get-tuple-element.14), channel_id=1, source_target_pairs={{16,0},{32,16},{48,32},{64,48},{80,64},{96,80},{112,96},{128,112},... | collective-permute-start | bytes 58376 | tf_op jit(solution)/shard_map/ppermute | solution.py:20
  144.3 5.1 %collective-permute-start.1 = (f32[38,1,128]{2,1,0:T(1,128)S(1)}, f32[38,1,128]{2,1,0:T(1,128)S(1)}, u32[]{:S(2)}, u32[]{:S(2)}) collective-permute-start(f32[38,1,128]{2,1,0:T(1,128)S(1)} %get-tuple-element.15), channel_id=1, source_target_pairs={{0,16},{16,32},{32,48},{48,64},{64,80},{80,96},{96,112},{112,128},... | collective-permute-start | bytes 58376 | tf_op jit(solution)/shard_map/ppermute | solution.py:17
  150.0 6.1 %collective-permute-start.2 = (f32[38,1,128]{2,1,0:T(1,128)S(1)}, f32[38,1,128]{2,1,0:T(1,128)S(1)}, u32[]{:S(2)}, u32[]{:S(2)}) collective-permute-start(f32[38,1,128]{2,1,0:T(1,128)S(1)} %get-tuple-element.12), channel_id=1, source_target_pairs={{16,0},{32,16},{48,32},{64,48},{80,64},{96,80},{112,96},{128,112},... | collective-permute-start | bytes 58376 | tf_op jit(solution)/shard_map/ppermute | solution.py:20
  151.9 5.1 %collective-permute-start.3 = (f32[38,1,128]{2,1,0:T(1,128)S(1)}, f32[38,1,128]{2,1,0:T(1,128)S(1)}, u32[]{:S(2)}, u32[]{:S(2)}) collective-permute-start(f32[38,1,128]{2,1,0:T(1,128)S(1)} %get-tuple-element.13), channel_id=1, source_target_pairs={{0,16},{16,32},{32,48},{48,64},{64,80},{80,96},{96,112},{112,128},... | collective-permute-start | bytes 58376 | tf_op jit(solution)/shard_map/ppermute | solution.py:17
  157.6 6.1 %collective-permute-start.4 = (f32[38,1,128]{2,1,0:T(1,128)S(1)}, f32[38,1,128]{2,1,0:T(1,128)S(1)}, u32[]{:S(2)}, u32[]{:S(2)}) collective-permute-start(f32[38,1,128]{2,1,0:T(1,128)S(1)} %get-tuple-element.10), channel_id=1, source_target_pairs={{16,0},{32,16},{48,32},{64,48},{80,64},{96,80},{112,96},{128,112},... | collective-permute-start | bytes 58376 | tf_op jit(solution)/shard_map/ppermute | solution.py:20
  159.5 5.1 %collective-permute-start.5 = (f32[38,1,128]{2,1,0:T(1,128)S(1)}, f32[38,1,128]{2,1,0:T(1,128)S(1)}, u32[]{:S(2)}, u32[]{:S(2)}) collective-permute-start(f32[38,1,128]{2,1,0:T(1,128)S(1)} %get-tuple-element.11), channel_id=1, source_target_pairs={{0,16},{16,32},{32,48},{48,64},{64,80},{80,96},{96,112},{112,128},... | collective-permute-start | bytes 58376 | tf_op jit(solution)/shard_map/ppermute | solution.py:17
  166.2 74.8 %copy-start.3 = (bf16[38,608]{1,0:T(8,128)(2,1)S(1)}, bf16[38,608]{1,0:T(8,128)(2,1)}, u32[]{:S(2)}) copy-start(bf16[38,608]{1,0:T(8,128)(2,1)} %param.15) | copy-start | bytes 138628
Sparse Core Ops, SparseCore 0:
  166.3 68.8 all-gather.2
where the time goes:
time: 253 us; the launch traced here: 252 us
  waiting for transfers between devices  170 us (67%)
  starting transfers between devices  36.2 us (14%)
  local copies, waits for them, and re-layouts  22.4 us (9%)
  between operations  13.6 us (5%)
  other arithmetic  5.22 us (2%)
  matrix products  4.96 us (2%)
    all_to_all x1, waiting for transfers between devices, on_device(): lax.all_to_all(outgoing, 'swath', split_axis=0, concat_axis=0, tiled=True)  97.9 us
    all_gather x1, waiting for transfers between devices, on_device(): lax.all_gather(smoothed, 'chan', axis=0, tiled=True)  69 us
    all_to_all x1, starting transfers between devices, on_device(): lax.all_to_all(outgoing, 'swath', split_axis=0, concat_axis=0, tiled=True)  16.9 us
    gather x1, local copies, waits for them, and re-layouts, on_device(): grid_profiles[slot_rows]  14.6 us
    ppermute x3, starting transfers between devices, extended_2(): lax.ppermute(lax.slice_in_dim(block, block.shape[dim] - width, None, axis...  12.6 us
    unnamed x18, local copies, waits for them, and re-layouts  7.56 us
    ppermute x3, starting transfers between devices, extended_2(): lax.ppermute(lax.slice_in_dim(block, 0, width, axis=dim), axis, backward)  6.62 us
  transfers between devices with their start and end apart: 8, of which 5 were waited for; matrix products, arithmetic and copies ran while one was open for 0% of the time, Pallas kernels for 0%

commit v1 on v0

--- a/solution.py
+++ b/solution.py
@@ -7,6 +7,27 @@
 XTRACK = 128
 NANG = 8
 max_zenith = math.pi / 3.0
+
+
+def ring_gather(array, axis, dim):
+    size, position, rows = (lax.axis_size(axis), lax.axis_index(axis), array.shape[dim])
+    upward = [(i, (i + 1) % size) for i in range(size)]
+    backward = [(i, (i - 1) % size) for i in range(size)]
+    result = jnp.zeros((*array.shape[:dim], size * rows, *array.shape[dim + 1 :]), array.dtype)
+    result = lax.dynamic_update_slice_in_dim(result, array, position * rows, axis=dim)
+    from_left = from_right = array
+    half = size // 2
+    for turn in range(1, half + 1):
+        from_left = lax.ppermute(from_left, axis, upward)
+        result = lax.dynamic_update_slice_in_dim(
+            result, from_left, (position - turn) % size * rows, axis=dim
+        )
+        if turn < size - half:
+            from_right = lax.ppermute(from_right, axis, backward)
+            result = lax.dynamic_update_slice_in_dim(
+                result, from_right, (position + turn) % size * rows, axis=dim
+            )
+    return result
 
 
 def extended_2(block, sides, width):
@@ -58,11 +79,7 @@
     for sweep in range(3):
         smooth_field = diffuse_once(line_rims(smooth_field), along_rate, cross_rate)
     smoothed = smooth_field.reshape(own_chan, pixel_count).astype(jnp.bfloat16)
-    return jnp.dot(
-        factor,
-        lax.all_gather(smoothed, "chan", axis=0, tiled=True),
-        preferred_element_type=jnp.float32,
-    )
+    return jnp.dot(factor, ring_gather(smoothed, "chan", 0), preferred_element_type=jnp.float32)
 
 
 def solution(mesh):

time: 253 us -> 308 us (1.22); the launches traced: 252 us -> 303 us
  starting transfers between devices: 36.2 us -> 101 us
  waiting for transfers between devices: 170 us -> 128 us
  local copies, waits for them, and re-layouts: 22.4 us -> 63.3 us
  between operations: 13.6 us -> 0.78 us
    all_gather x1 -> x0, waiting for transfers between devices: 69 us -> none  [on_device(): lax.all_gather(smoothed, 'chan', axis=0, tiled=True)]
    ppermute x0 -> x15, starting transfers between devices: none -> 64.7 us  [the longest x7 48.1 us: ring_gather(): from_right = lax.ppermute(from_right, axis, backward)]
    dynamic_update_slice x0 -> x16, local copies, waits for them, and re-layouts: none -> 44.9 us  [the longest x8 22.4 us: ring_gather(): lax.dynamic_update_slice_in_dim(result, from_left, (position - turn) % si...]
    ppermute x0 -> x15, waiting for transfers between devices: none -> 27 us  [the longest x8 26.8 us: ring_gather(): from_left = lax.ppermute(from_left, axis, upward)]
    unnamed x18 -> x30, local copies, waits for them, and re-layouts: 7.56 us -> 0.69 us
  transfers between devices with their start and end apart: 8 -> 22, of which waited for: 5 -> 12; matrix products, arithmetic and copies ran while one was open for 0% -> 15% of each run, Pallas kernels for 0% -> 0%
where the time goes in v1:
time: 308 us; the launch traced here: 303 us
  waiting for transfers between devices  128 us (42%)
  starting transfers between devices  101 us (33%)
  local copies, waits for them, and re-layouts  63.3 us (21%)
  other arithmetic  5.25 us (2%)
  matrix products  4.96 us (2%)
    all_to_all x1, waiting for transfers between devices, on_device(): lax.all_to_all(outgoing, 'swath', split_axis=0, concat_axis=0, tiled=True)  98.4 us
    ppermute x7, starting transfers between devices, ring_gather(): from_right = lax.ppermute(from_right, axis, backward)  48.1 us
    ppermute x8, waiting for transfers between devices, ring_gather(): from_left = lax.ppermute(from_left, axis, upward)  26.8 us
    dynamic_update_slice x8, local copies, waits for them, and re-layouts, ring_gather(): lax.dynamic_update_slice_in_dim(result, from_left, (position - turn) % si...  22.4 us
    dynamic_update_slice x7, local copies, waits for them, and re-layouts, ring_gather(): lax.dynamic_update_slice_in_dim(result, from_right, (position + turn) % s...  19.7 us
    all_to_all x1, starting transfers between devices, on_device(): lax.all_to_all(outgoing, 'swath', split_axis=0, concat_axis=0, tiled=True)  16.7 us
    ppermute x8, starting transfers between devices, ring_gather(): from_left = lax.ppermute(from_left, axis, upward)  16.6 us
    gather x1, local copies, waits for them, and re-layouts, on_device(): grid_profiles[slot_rows]  14.6 us
  transfers between devices with their start and end apart: 22, of which 12 were waited for; matrix products, arithmetic and copies ran while one was open for 15% of the time, Pallas kernels for 0%

profile of v1, /device:TPU:1, one launch (start us, length us, event | category | flops | bytes accessed | tf_op | source)
XLA Modules:
  0.0 303.0 jit_solution(18331730285552362905)
XLA Ops:
  1.5 14.6 %gather_fusion = bf16[4096,256]{1,0:T(8,128)(2,1)S(1)} fusion(bf16[1024,256]{1,0:T(8,128)(2,1)S(1)} %copy-done, s32[4096]{0:T(1024)S(1)} %fusion.29), kind=kCustom, calls=%fused_computation | custom fusion | bytes 4210688 | tf_op jit(solution)/shard_map/gather | solution.py:66
  17.9 16.7 %all-to-all-start = ((bf16[32,128,256]{2,1,0:T(8,128)(2,1)}), bf16[32,128,256]{2,1,0:T(8,128)(2,1)S(1)}, u32[]{:S(2)}, u32[]{:S(2)}) async-start(bf16[32,128,256]{2,1,0:T(8,128)(2,1)} %broadcast_select_fusion), calls=%async_computation | async-start | bytes 4194304 | tf_op jit(solution)/shard_map/all_to_all | solution.py:67
  34.9 98.4 %all-to-all-done = bf16[32,128,256]{2,1,0:T(8,128)(2,1)S(1)} async-done(((bf16[32,128,256]{2,1,0:T(8,128)(2,1)}), bf16[32,128,256]{2,1,0:T(8,128)(2,1)S(1)}, u32[]{:S(2)}, u32[]{:S(2)}) %all-to-all-start) | async-done | bytes 2097184 | tf_op jit(solution)/shard_map/all_to_all | solution.py:67
  137.7 4.2 %collective-permute-start.1 = (f32[38,1,128]{2,1,0:T(1,128)S(1)}, f32[38,1,128]{2,1,0:T(1,128)S(1)}, u32[]{:S(2)}, u32[]{:S(2)}) collective-permute-start(f32[38,1,128]{2,1,0:T(1,128)S(1)} %get-tuple-element.15), channel_id=1, source_target_pairs={{0,16},{16,32},{32,48},{48,64},{64,80},{80,96},{96,112},{112,128},... | collective-permute-start | bytes 58376 | tf_op jit(solution)/shard_map/ppermute | solution.py:38
  145.3 4.2 %collective-permute-start.3 = (f32[38,1,128]{2,1,0:T(1,128)S(1)}, f32[38,1,128]{2,1,0:T(1,128)S(1)}, u32[]{:S(2)}, u32[]{:S(2)}) collective-permute-start(f32[38,1,128]{2,1,0:T(1,128)S(1)} %get-tuple-element.13), channel_id=1, source_target_pairs={{0,16},{16,32},{32,48},{48,64},{64,80},{80,96},{96,112},{112,128},... | collective-permute-start | bytes 58376 | tf_op jit(solution)/shard_map/ppermute | solution.py:38
  152.9 4.2 %collective-permute-start.5 = (f32[38,1,128]{2,1,0:T(1,128)S(1)}, f32[38,1,128]{2,1,0:T(1,128)S(1)}, u32[]{:S(2)}, u32[]{:S(2)}) collective-permute-start(f32[38,1,128]{2,1,0:T(1,128)S(1)} %get-tuple-element.11), channel_id=1, source_target_pairs={{0,16},{16,32},{32,48},{48,64},{64,80},{80,96},{96,112},{112,128},... | collective-permute-start | bytes 58376 | tf_op jit(solution)/shard_map/ppermute | solution.py:38
  158.8 3.2 %collective-permute-start.6 = (bf16[38,4096]{1,0:T(8,128)(2,1)S(1)}, bf16[38,4096]{1,0:T(8,128)(2,1)S(1)}, u32[]{:S(2)}, u32[]{:S(2)}) collective-permute-start(bf16[38,4096]{1,0:T(8,128)(2,1)S(1)} %bitcast.51), channel_id=1, source_target_pairs={{0,1},{1,2},{2,3},{3,4},{4,5},{5,6},{6,7},{7,8},{8,9},{9,10},{10,1... | collective-permute-start | bytes 933896 | tf_op jit(solution)/shard_map/ppermute | solution.py:21
  162.0 5.6 %collective-permute-start.7 = (bf16[38,4096]{1,0:T(8,128)(2,1)S(1)}, bf16[38,4096]{1,0:T(8,128)(2,1)S(1)}, u32[]{:S(2)}, u32[]{:S(2)}) collective-permute-start(bf16[38,4096]{1,0:T(8,128)(2,1)S(1)} %bitcast.52), channel_id=1, source_target_pairs={{0,15},{1,0},{2,1},{3,2},{4,3},{5,4},{6,5},{7,6},{8,7},{9,8},{10,9... | collective-permute-start | bytes 933896 | tf_op jit(solution)/shard_map/ppermute | solution.py:26
  167.6 4.5 %collective-permute-done.6 = bf16[38,4096]{1,0:T(8,128)(2,1)S(1)} collective-permute-done((bf16[38,4096]{1,0:T(8,128)(2,1)S(1)}, bf16[38,4096]{1,0:T(8,128)(2,1)S(1)}, u32[]{:S(2)}, u32[]{:S(2)}) %collective-permute-start.6) | collective-permute-done | bytes 311328 | tf_op jit(solution)/shard_map/ppermute | solution.py:21
  174.0 7.0 %collective-permute-start.9 = (bf16[38,4096]{1,0:T(8,128)(2,1)S(1)}, bf16[38,4096]{1,0:T(8,128)(2,1)S(1)}, u32[]{:S(2)}, u32[]{:S(2)}) collective-permute-start(bf16[38,4096]{1,0:T(8,128)(2,1)S(1)} %collective-permute-done.7), channel_id=1, source_target_pairs={{0,15},{1,0},{2,1},{3,2},{4,3},{5,4},{6,5},{7,6},{8,7},{9,8},{10,9... | collective-permute-start | bytes 933896 | tf_op jit(solution)/shard_map/ppermute | solution.py:26
  180.9 5.3 %collective-permute-done.8 = bf16[38,4096]{1,0:T(8,128)(2,1)S(1)} collective-permute-done((bf16[38,4096]{1,0:T(8,128)(2,1)S(1)}, bf16[38,4096]{1,0:T(8,128)(2,1)S(1)}, u32[]{:S(2)}, u32[]{:S(2)}) %collective-permute-start.8) | collective-permute-done | bytes 311328 | tf_op jit(solution)/shard_map/ppermute | solution.py:21
  188.3 7.2 %collective-permute-start.11 = (bf16[38,4096]{1,0:T(8,128)(2,1)S(1)}, bf16[38,4096]{1,0:T(8,128)(2,1)S(1)}, u32[]{:S(2)}, u32[]{:S(2)}) collective-permute-start(bf16[38,4096]{1,0:T(8,128)(2,1)S(1)} %collective-permute-done.9), channel_id=1, source_target_pairs={{0,15},{1,0},{2,1},{3,2},{4,3},{5,4},{6,5},{7,6},{8,7},{9,8},{10,9... | collective-permute-start | bytes 933896 | tf_op jit(solution)/shard_map/ppermute | solution.py:26
  195.6 4.9 %collective-permute-done.10 = bf16[38,4096]{1,0:T(8,128)(2,1)S(1)} collective-permute-done((bf16[38,4096]{1,0:T(8,128)(2,1)S(1)}, bf16[38,4096]{1,0:T(8,128)(2,1)S(1)}, u32[]{:S(2)}, u32[]{:S(2)}) %collective-permute-start.10) | collective-permute-done | bytes 311328 | tf_op jit(solution)/shard_map/ppermute | solution.py:21
  202.4 7.3 %collective-permute-start.13 = (bf16[38,4096]{1,0:T(8,128)(2,1)S(1)}, bf16[38,4096]{1,0:T(8,128)(2,1)S(1)}, u32[]{:S(2)}, u32[]{:S(2)}) collective-permute-start(bf16[38,4096]{1,0:T(8,128)(2,1)S(1)} %collective-permute-done.11), channel_id=1, source_target_pairs={{0,15},{1,0},{2,1},{3,2},{4,3},{5,4},{6,5},{7,6},{8,7},{9,8},{10,9... | collective-permute-start | bytes 933896 | tf_op jit(solution)/shard_map/ppermute | solution.py:26
  209.7 4.1 %collective-permute-done.12 = bf16[38,4096]{1,0:T(8,128)(2,1)S(1)} collective-permute-done((bf16[38,4096]{1,0:T(8,128)(2,1)S(1)}, bf16[38,4096]{1,0:T(8,128)(2,1)S(1)}, u32[]{:S(2)}, u32[]{:S(2)}) %collective-permute-start.12) | collective-permute-done | bytes 311328 | tf_op jit(solution)/shard_map/ppermute | solution.py:21
  215.7 7.2 %collective-permute-start.15 = (bf16[38,4096]{1,0:T(8,128)(2,1)S(1)}, bf16[38,4096]{1,0:T(8,128)(2,1)S(1)}, u32[]{:S(2)}, u32[]{:S(2)}) collective-permute-start(bf16[38,4096]{1,0:T(8,128)(2,1)S(1)} %collective-permute-done.13), channel_id=1, source_target_pairs={{0,15},{1,0},{2,1},{3,2},{4,3},{5,4},{6,5},{7,6},{8,7},{9,8},{10,9... | collective-permute-start | bytes 933896 | tf_op jit(solution)/shard_map/ppermute | solution.py:26
  222.9 3.2 %collective-permute-done.14 = bf16[38,4096]{1,0:T(8,128)(2,1)S(1)} collective-permute-done((bf16[38,4096]{1,0:T(8,128)(2,1)S(1)}, bf16[38,4096]{1,0:T(8,128)(2,1)S(1)}, u32[]{:S(2)}, u32[]{:S(2)}) %collective-permute-start.14) | collective-permute-done | bytes 311328 | tf_op jit(solution)/shard_map/ppermute | solution.py:21
  228.1 7.1 %collective-permute-start.17 = (bf16[38,4096]{1,0:T(8,128)(2,1)S(1)}, bf16[38,4096]{1,0:T(8,128)(2,1)}, u32[]{:S(2)}, u32[]{:S(2)}) collective-permute-start(bf16[38,4096]{1,0:T(8,128)(2,1)S(1)} %collective-permute-done.15), channel_id=1, source_target_pairs={{0,15},{1,0},{2,1},{3,2},{4,3},{5,4},{6,5},{7,6},{8,7},{9,8},{10,9... | collective-permute-start | bytes 933896 | tf_op jit(solution)/shard_map/ppermute | solution.py:26
  239.5 6.9 %collective-permute-start.19 = (bf16[38,4096]{1,0:T(8,128)(2,1)}, bf16[38,4096]{1,0:T(8,128)(2,1)}, u32[]{:S(2)}, u32[]{:S(2)}) collective-permute-start(bf16[38,4096]{1,0:T(8,128)(2,1)} %collective-permute-done.17), channel_id=1, source_target_pairs={{0,15},{1,0},{2,1},{3,2},{4,3},{5,4},{6,5},{7,6},{8,7},{9,8},{10,9... | collective-permute-start | bytes 933896 | tf_op jit(solution)/shard_map/ppermute | solution.py:26
  287.1 2.9 dynamic_update_slice.60
  290.0 2.9 dynamic_update_slice.61
  292.9 2.9 dynamic_update_slice.62
  295.9 2.9 dynamic_update_slice.63
  298.8 4.2 %convolution_bitcast_fusion.1 = f32[38,4096]{1,0:T(8,128)} fusion(bf16[608,4096]{1,0:T(8,128)(2,1)} %dynamic_update_slice.63, bf16[38,608]{1,0:T(8,128)(2,1)S(1)} %copy-done.9), kind=kOutput, calls=%fused_computation.2 | convolution fusion | flops 189267968 | bytes 5649536 | tf_op jit(solution)/shard_map/dot_general | solution.py:82
  (84 shorter events, 70.7 us)
Async XLA Ops:
  16.2 117.1 %copy-start.8 = (bf16[3,256,38]{1,2,0:T(8,128)(2,1)S(1)}, bf16[3,256,38]{1,2,0:T(8,128)(2,1)}, u32[]{:S(2)}) copy-start(bf16[3,256,38]{1,2,0:T(8,128)(2,1)} %param.12) | copy-start | bytes 175108
  17.9 115.4 %all-to-all-start = ((bf16[32,128,256]{2,1,0:T(8,128)(2,1)}), bf16[32,128,256]{2,1,0:T(8,128)(2,1)S(1)}, u32[]{:S(2)}, u32[]{:S(2)}) async-start(bf16[32,128,256]{2,1,0:T(8,128)(2,1)} %broadcast_select_fusion), calls=%async_computation | async-start | bytes 4194304 | tf_op jit(solution)/shard_map/all_to_all | solution.py:67
  135.0 7.0 %collective-permute-start = (f32[38,1,128]{2,1,0:T(1,128)S(1)}, f32[38,1,128]{2,1,0:T(1,128)S(1)}, u32[]{:S(2)}, u32[]{:S(2)}) collective-permute-start(f32[38,1,128]{2,1,0:T(1,128)S(1)} %get-tuple-element.14), channel_id=1, source_target_pairs={{16,0},{32,16},{48,32},{64,48},{80,64},{96,80},{112,96},{128,112},... | collective-permute-start | bytes 58376 | tf_op jit(solution)/shard_map/ppermute | solution.py:41
  137.7 5.1 %collective-permute-start.1 = (f32[38,1,128]{2,1,0:T(1,128)S(1)}, f32[38,1,128]{2,1,0:T(1,128)S(1)}, u32[]{:S(2)}, u32[]{:S(2)}) collective-permute-start(f32[38,1,128]{2,1,0:T(1,128)S(1)} %get-tuple-element.15), channel_id=1, source_target_pairs={{0,16},{16,32},{32,48},{48,64},{64,80},{80,96},{96,112},{112,128},... | collective-permute-start | bytes 58376 | tf_op jit(solution)/shard_map/ppermute | solution.py:38
  143.4 6.1 %collective-permute-start.2 = (f32[38,1,128]{2,1,0:T(1,128)S(1)}, f32[38,1,128]{2,1,0:T(1,128)S(1)}, u32[]{:S(2)}, u32[]{:S(2)}) collective-permute-start(f32[38,1,128]{2,1,0:T(1,128)S(1)} %get-tuple-element.12), channel_id=1, source_target_pairs={{16,0},{32,16},{48,32},{64,48},{80,64},{96,80},{112,96},{128,112},... | collective-permute-start | bytes 58376 | tf_op jit(solution)/shard_map/ppermute | solution.py:41
  145.3 5.1 %collective-permute-start.3 = (f32[38,1,128]{2,1,0:T(1,128)S(1)}, f32[38,1,128]{2,1,0:T(1,128)S(1)}, u32[]{:S(2)}, u32[]{:S(2)}) collective-permute-start(f32[38,1,128]{2,1,0:T(1,128)S(1)} %get-tuple-element.13), channel_id=1, source_target_pairs={{0,16},{16,32},{32,48},{48,64},{64,80},{80,96},{96,112},{112,128},... | collective-permute-start | bytes 58376 | tf_op jit(solution)/shard_map/ppermute | solution.py:38
  151.0 6.1 %collective-permute-start.4 = (f32[38,1,128]{2,1,0:T(1,128)S(1)}, f32[38,1,128]{2,1,0:T(1,128)S(1)}, u32[]{:S(2)}, u32[]{:S(2)}) collective-permute-start(f32[38,1,128]{2,1,0:T(1,128)S(1)} %get-tuple-element.10), channel_id=1, source_target_pairs={{16,0},{32,16},{48,32},{64,48},{80,64},{96,80},{112,96},{128,112},... | collective-permute-start | bytes 58376 | tf_op jit(solution)/shard_map/ppermute | solution.py:41
  152.9 5.1 %collective-permute-start.5 = (f32[38,1,128]{2,1,0:T(1,128)S(1)}, f32[38,1,128]{2,1,0:T(1,128)S(1)}, u32[]{:S(2)}, u32[]{:S(2)}) collective-permute-start(f32[38,1,128]{2,1,0:T(1,128)S(1)} %get-tuple-element.11), channel_id=1, source_target_pairs={{0,16},{16,32},{32,48},{48,64},{64,80},{80,96},{96,112},{112,128},... | collective-permute-start | bytes 58376 | tf_op jit(solution)/shard_map/ppermute | solution.py:38
  158.8 13.3 %collective-permute-start.6 = (bf16[38,4096]{1,0:T(8,128)(2,1)S(1)}, bf16[38,4096]{1,0:T(8,128)(2,1)S(1)}, u32[]{:S(2)}, u32[]{:S(2)}) collective-permute-start(bf16[38,4096]{1,0:T(8,128)(2,1)S(1)} %bitcast.51), channel_id=1, source_target_pairs={{0,1},{1,2},{2,3},{3,4},{4,5},{5,6},{6,7},{7,8},{8,9},{9,10},{10,1... | collective-permute-start | bytes 933896 | tf_op jit(solution)/shard_map/ppermute | solution.py:21
  162.0 12.0 %collective-permute-start.7 = (bf16[38,4096]{1,0:T(8,128)(2,1)S(1)}, bf16[38,4096]{1,0:T(8,128)(2,1)S(1)}, u32[]{:S(2)}, u32[]{:S(2)}) collective-permute-start(bf16[38,4096]{1,0:T(8,128)(2,1)S(1)} %bitcast.52), channel_id=1, source_target_pairs={{0,15},{1,0},{2,1},{3,2},{4,3},{5,4},{6,5},{7,6},{8,7},{9,8},{10,9... | collective-permute-start | bytes 933896 | tf_op jit(solution)/shard_map/ppermute | solution.py:26
  172.1 14.2 %collective-permute-start.8 = (bf16[38,4096]{1,0:T(8,128)(2,1)S(1)}, bf16[38,4096]{1,0:T(8,128)(2,1)S(1)}, u32[]{:S(2)}, u32[]{:S(2)}) collective-permute-start(bf16[38,4096]{1,0:T(8,128)(2,1)S(1)} %collective-permute-done.6), channel_id=1, source_target_pairs={{0,1},{1,2},{2,3},{3,4},{4,5},{5,6},{6,7},{7,8},{8,9},{9,10},{10,1... | collective-permute-start | bytes 933896 | tf_op jit(solution)/shard_map/ppermute | solution.py:21
  174.0 14.3 %collective-permute-start.9 = (bf16[38,4096]{1,0:T(8,128)(2,1)S(1)}, bf16[38,4096]{1,0:T(8,128)(2,1)S(1)}, u32[]{:S(2)}, u32[]{:S(2)}) collective-permute-start(bf16[38,4096]{1,0:T(8,128)(2,1)S(1)} %collective-permute-done.7), channel_id=1, source_target_pairs={{0,15},{1,0},{2,1},{3,2},{4,3},{5,4},{6,5},{7,6},{8,7},{9,8},{10,9... | collective-permute-start | bytes 933896 | tf_op jit(solution)/shard_map/ppermute | solution.py:26
  186.2 14.2 %collective-permute-start.10 = (bf16[38,4096]{1,0:T(8,128)(2,1)S(1)}, bf16[38,4096]{1,0:T(8,128)(2,1)S(1)}, u32[]{:S(2)}, u32[]{:S(2)}) collective-permute-start(bf16[38,4096]{1,0:T(8,128)(2,1)S(1)} %collective-permute-done.8), channel_id=1, source_target_pairs={{0,1},{1,2},{2,3},{3,4},{4,5},{5,6},{6,7},{7,8},{8,9},{9,10},{10,1... | collective-permute-start | bytes 933896 | tf_op jit(solution)/shard_map/ppermute | solution.py:21
  188.3 14.0 %collective-permute-start.11 = (bf16[38,4096]{1,0:T(8,128)(2,1)S(1)}, bf16[38,4096]{1,0:T(8,128)(2,1)S(1)}, u32[]{:S(2)}, u32[]{:S(2)}) collective-permute-start(bf16[38,4096]{1,0:T(8,128)(2,1)S(1)} %collective-permute-done.9), channel_id=1, source_target_pairs={{0,15},{1,0},{2,1},{3,2},{4,3},{5,4},{6,5},{7,6},{8,7},{9,8},{10,9... | collective-permute-start | bytes 933896 | tf_op jit(solution)/shard_map/ppermute | solution.py:26
  200.4 13.3 %collective-permute-start.12 = (bf16[38,4096]{1,0:T(8,128)(2,1)S(1)}, bf16[38,4096]{1,0:T(8,128)(2,1)S(1)}, u32[]{:S(2)}, u32[]{:S(2)}) collective-permute-start(bf16[38,4096]{1,0:T(8,128)(2,1)S(1)} %collective-permute-done.10), channel_id=1, source_target_pairs={{0,1},{1,2},{2,3},{3,4},{4,5},{5,6},{6,7},{7,8},{8,9},{9,10},{10,1... | collective-permute-start | bytes 933896 | tf_op jit(solution)/shard_map/ppermute | solution.py:21
  202.4 13.3 %collective-permute-start.13 = (bf16[38,4096]{1,0:T(8,128)(2,1)S(1)}, bf16[38,4096]{1,0:T(8,128)(2,1)S(1)}, u32[]{:S(2)}, u32[]{:S(2)}) collective-permute-start(bf16[38,4096]{1,0:T(8,128)(2,1)S(1)} %collective-permute-done.11), channel_id=1, source_target_pairs={{0,15},{1,0},{2,1},{3,2},{4,3},{5,4},{6,5},{7,6},{8,7},{9,8},{10,9... | collective-permute-start | bytes 933896 | tf_op jit(solution)/shard_map/ppermute | solution.py:26
  213.7 12.4 %collective-permute-start.14 = (bf16[38,4096]{1,0:T(8,128)(2,1)S(1)}, bf16[38,4096]{1,0:T(8,128)(2,1)S(1)}, u32[]{:S(2)}, u32[]{:S(2)}) collective-permute-start(bf16[38,4096]{1,0:T(8,128)(2,1)S(1)} %collective-permute-done.12), channel_id=1, source_target_pairs={{0,1},{1,2},{2,3},{3,4},{4,5},{5,6},{6,7},{7,8},{8,9},{9,10},{10,1... | collective-permute-start | bytes 933896 | tf_op jit(solution)/shard_map/ppermute | solution.py:21
  215.7 12.4 %collective-permute-start.15 = (bf16[38,4096]{1,0:T(8,128)(2,1)S(1)}, bf16[38,4096]{1,0:T(8,128)(2,1)S(1)}, u32[]{:S(2)}, u32[]{:S(2)}) collective-permute-start(bf16[38,4096]{1,0:T(8,128)(2,1)S(1)} %collective-permute-done.13), channel_id=1, source_target_pairs={{0,15},{1,0},{2,1},{3,2},{4,3},{5,4},{6,5},{7,6},{8,7},{9,8},{10,9... | collective-permute-start | bytes 933896 | tf_op jit(solution)/shard_map/ppermute | solution.py:26
  226.1 11.4 %collective-permute-start.16 = (bf16[38,4096]{1,0:T(8,128)(2,1)S(1)}, bf16[38,4096]{1,0:T(8,128)(2,1)S(1)}, u32[]{:S(2)}, u32[]{:S(2)}) collective-permute-start(bf16[38,4096]{1,0:T(8,128)(2,1)S(1)} %collective-permute-done.14), channel_id=1, source_target_pairs={{0,1},{1,2},{2,3},{3,4},{4,5},{5,6},{6,7},{7,8},{8,9},{9,10},{10,1... | collective-permute-start | bytes 933896 | tf_op jit(solution)/shard_map/ppermute | solution.py:21
  228.1 11.4 %collective-permute-start.17 = (bf16[38,4096]{1,0:T(8,128)(2,1)S(1)}, bf16[38,4096]{1,0:T(8,128)(2,1)}, u32[]{:S(2)}, u32[]{:S(2)}) collective-permute-start(bf16[38,4096]{1,0:T(8,128)(2,1)S(1)} %collective-permute-done.15), channel_id=1, source_target_pairs={{0,15},{1,0},{2,1},{3,2},{4,3},{5,4},{6,5},{7,6},{8,7},{9,8},{10,9... | collective-permute-start | bytes 933896 | tf_op jit(solution)/shard_map/ppermute | solution.py:26
  237.6 11.2 %collective-permute-start.18 = (bf16[38,4096]{1,0:T(8,128)(2,1)S(1)}, bf16[38,4096]{1,0:T(8,128)(2,1)}, u32[]{:S(2)}, u32[]{:S(2)}) collective-permute-start(bf16[38,4096]{1,0:T(8,128)(2,1)S(1)} %collective-permute-done.16), channel_id=1, source_target_pairs={{0,1},{1,2},{2,3},{3,4},{4,5},{5,6},{6,7},{7,8},{8,9},{9,10},{10,1... | collective-permute-start | bytes 933896 | tf_op jit(solution)/shard_map/ppermute | solution.py:21
  239.5 53.5 %collective-permute-start.19 = (bf16[38,4096]{1,0:T(8,128)(2,1)}, bf16[38,4096]{1,0:T(8,128)(2,1)}, u32[]{:S(2)}, u32[]{:S(2)}) collective-permute-start(bf16[38,4096]{1,0:T(8,128)(2,1)} %collective-permute-done.17), channel_id=1, source_target_pairs={{0,15},{1,0},{2,1},{3,2},{4,3},{5,4},{6,5},{7,6},{8,7},{9,8},{10,9... | collective-permute-start | bytes 933896 | tf_op jit(solution)/shard_map/ppermute | solution.py:26
  248.8 47.1 %collective-permute-start.20 = (bf16[38,4096]{1,0:T(8,128)(2,1)}, bf16[38,4096]{1,0:T(8,128)(2,1)}, u32[]{:S(2)}, u32[]{:S(2)}) collective-permute-start(bf16[38,4096]{1,0:T(8,128)(2,1)} %collective-permute-done.18), channel_id=1, source_target_pairs={{0,1},{1,2},{2,3},{3,4},{4,5},{5,6},{6,7},{7,8},{8,9},{9,10},{10,1... | collective-permute-start | bytes 933896 | tf_op jit(solution)/shard_map/ppermute | solution.py:21
  256.7 42.1 %copy-start.9 = (bf16[38,608]{1,0:T(8,128)(2,1)S(1)}, bf16[38,608]{1,0:T(8,128)(2,1)}, u32[]{:S(2)}) copy-start(bf16[38,608]{1,0:T(8,128)(2,1)} %param.15) | copy-start | bytes 138628
  (10 other events, 126.4 us)
